TPU v7x, 128 devices: a whole 4x4x4 slice. The times are simulated.
128 devices in a mesh: ep: 4 (over x), tm: 32 (over y, z, core).
Axes of the slice: x: 4, y: 4, z: 4, core: 2. Of those that a mesh axis runs over, the one named last changes fastest.
Arguments:
- predictions: float32 [128, 1048576], P('ep', 'tm'), may hold values from -6 to 6
- leaf_index: int32 [128, 1048576], P('ep', 'tm'), may hold values from 0 to 63
- events: int32 [128, 1048576], P('ep', 'tm'), may hold values 0 or 1
- tie_start: int32 [1048576], P('tm'), may hold values from 0 to 1, as said below
Outputs:
- new_pred: float32 [128, 1048576], P('ep', 'tm')
- leaf_weights: float32 [128, 64], P('ep')
- grad_hess: bfloat16 [2, 128, 32, 32768], P(None, None, 'tm', 'ep')
Inputs may be any that keep to these rules, and one draw needn't show every extreme that they name: `tie_start`: every row whose index is a multiple of 128 begins a tie group.
All inputs are finite; a program needn't handle non-finite values. No bound on the sum of `events` on one device may be relied on, other than what follows from the above.
Results may differ from a plain program's by a relative error of at most 0.0023.
Values may be sent and summed in bfloat16 or wider, within the bound.
A program may use at most 128 MiB of HBM per device.

v0:
```python
import math
import jax
import jax.numpy as jnp
from jax import lax
from jax.sharding import PartitionSpec as P

LEAVES = 64


def prefix(part, axis, combine, identity, reverse):
    count = lax.axis_size(axis)
    place = lax.axis_index(axis)
    ahead = count - 1 - place if reverse else place
    gathered = jax.tree.map(lambda a: lax.all_gather(a, axis), part)
    state = jax.tree.map(lambda a, e: jnp.zeros_like(a) + jnp.asarray(e, a.dtype), part, identity)

    def one(turn, state):
        source = count - 1 - turn if reverse else turn
        return combine(
            state, jax.tree.map(lambda a: lax.dynamic_index_in_dim(a, source, 0, False), gathered)
        )

    return lax.fori_loop(0, ahead, one, state)


def tile_matrices(tie_start):
    length = tie_start.shape[0]
    blocks = length // 128
    starts = tie_start.reshape(blocks, 128)
    labels = jnp.arange(128, dtype=jnp.int32)
    first_local = lax.cummax(jnp.where(starts == 1, labels[None, :], 0), axis=1)
    next_start = jnp.concatenate([starts[:, 1:], jnp.ones((blocks, 1), jnp.int32)], axis=1)
    last_local = lax.cummin(jnp.where(next_start == 1, labels[None, :], 127), axis=1, reverse=True)
    backward = (labels[None, :, None] >= first_local[:, None, :]).astype(jnp.float32)
    forward = (labels[None, :, None] <= last_local[:, None, :]).astype(jnp.float32)
    return (backward, forward)


def block_cumsum(values, matrices, from_end):
    groups = values.shape[0]
    length = values.shape[1]
    blocks = length // 128
    shaped = values.reshape(groups, blocks, 128)
    within = jnp.einsum("ebj,bji->ebi", shaped, matrices, precision=lax.Precision.HIGHEST)
    totals = jnp.sum(shaped, axis=2)
    if from_end:
        offsets = jnp.cumsum(totals[:, ::-1], axis=1)[:, ::-1] - totals
    else:
        offsets = jnp.cumsum(totals, axis=1) - totals
    return (within + offsets[:, :, None]).reshape(groups, length)


def add_values(earlier, later):
    return jax.tree.map(lambda left, right: left + right, earlier, later)


def leaf_partials(leaf_index, gradient, hessian, leaves):
    length = leaf_index.shape[1]
    width = math.gcd(length, 2048)
    labels = jnp.arange(leaves, dtype=jnp.int32)

    def one_block(step, totals):
        start = step * width
        part_leaf = lax.dynamic_slice_in_dim(leaf_index, start, width, 1)
        part_grad = lax.dynamic_slice_in_dim(gradient, start, width, 1)
        part_hess = lax.dynamic_slice_in_dim(hessian, start, width, 1)
        hits = part_leaf[:, None, :] == labels[None, :, None]
        gsum = jnp.sum(jnp.where(hits, part_grad[:, None, :], 0.0), axis=2)
        hsum = jnp.sum(jnp.where(hits, part_hess[:, None, :], 0.0), axis=2)
        return totals + jnp.stack([gsum, hsum], axis=1)

    empty = jnp.zeros((leaf_index.shape[0], 2, leaves), jnp.float32)
    return lax.fori_loop(0, length // width, one_block, empty)


def leaf_lookup(leaf_index, table):
    length = leaf_index.shape[1]
    width = math.gcd(length, 2048)
    labels = jnp.arange(table.shape[1], dtype=jnp.int32)

    def one_block(step, result):
        start = step * width
        part_leaf = lax.dynamic_slice_in_dim(leaf_index, start, width, 1)
        hits = part_leaf[:, None, :] == labels[None, :, None]
        picked = jnp.sum(jnp.where(hits, table[:, :, None], 0.0), axis=1)
        return lax.dynamic_update_slice_in_dim(result, picked, start, 1)

    empty = jnp.zeros(leaf_index.shape, jnp.float32)
    return lax.fori_loop(0, length // width, one_block, empty)


def on_device(predictions, leaf_index, events, tie_start):
    groups = predictions.shape[0]
    length = predictions.shape[1]
    backward, forward = tile_matrices(tie_start)
    weight = jnp.exp(predictions)
    local_risk = block_cumsum(weight, backward, True)
    block_total = local_risk[:, 0]
    zero_column = jnp.zeros((groups,), jnp.float32)
    later_total = prefix(block_total, "tm", add_values, zero_column, True)
    risk = local_risk + later_total[:, None]
    observed = events.astype(jnp.float32)
    inv_one = observed / risk
    inv_two = inv_one / risk
    local_one = block_cumsum(inv_one, forward, False)
    local_two = block_cumsum(inv_two, forward, False)
    totals_pair = (local_one[:, -1], local_two[:, -1])
    earlier_one, earlier_two = prefix(
        totals_pair, "tm", add_values, (zero_column, zero_column), False
    )
    accum_one = local_one + earlier_one[:, None]
    accum_two = local_two + earlier_two[:, None]
    gradient = weight * accum_one - observed
    hessian = weight * accum_one - weight * weight * accum_two
    stacked = jnp.stack([gradient, hessian]).astype(jnp.bfloat16).reshape(2, groups, 1, length)
    grad_hess = lax.all_to_all(stacked, "ep", split_axis=3, concat_axis=1, tiled=True)
    partial_value = leaf_partials(leaf_index, gradient, hessian, LEAVES)
    totals = lax.psum(partial_value, "tm")
    leaf_weights = -totals[:, 0] / (totals[:, 1] + 1.0)
    new_pred = predictions + leaf_lookup(leaf_index, leaf_weights)
    return (new_pred, leaf_weights, grad_hess)


def solution(mesh):
    placed = (P("ep", "tm"), P("ep", "tm"), P("ep", "tm"), P("tm"))
    return jax.shard_map(
        on_device,
        mesh=mesh,
        in_specs=placed,
        out_specs=(P("ep", "tm"), P("ep", None), P(None, None, "tm", "ep")),
        check_vma=False,
    )
```

profile of v0, /device:TPU:2, one launch (start us, length us, event | category | flops | bytes accessed | tf_op | source)
XLA Modules:
  0.0 666.5 jit_solution(1025747727024494581)
XLA Ops:
  0.6 6.2 exponential_bitcast_fusion.1
  12.6 10.0 %fusion.22 = f32[256,4,8,128]{3,2,1,0:T(8,128)S(1)} fusion(f32[4,256,8,128]{3,2,1,0:T(8,128)} %get-tuple-element.397, s32[256,128]{1,0:T(8,128)S(1)} %copy.130, f32[32,256]{0,1:T(8,128)S(1)} %copy.134), kind=kOutput, calls=%fused_computation.44 | convolution fusion | flops 1615855616 | bytes 8552448 | tf_op jit(solution)/shard_map/ebj,bji->ebi/dot_general | solution.py:44
  26.2 68.6 %all-reduce.1 = f32[1024]{0:T(1024)S(1)} all-reduce(f32[1024]{0:T(1024)S(1)} %dynamic-update-slice), channel_id=2, replica_groups=mesh['ep'=4,'tm'=32] {'tm'}, use_global_device_ids=true, to_apply=%add.1 | all-reduce | flops 1024 | bytes 8192
  101.0 9.3 %fusion.34 = (f32[4,8,256,128]{3,1,2,0:T(8,128)}, f32[4,256,8,128]{3,2,1,0:T(8,128)}, f32[4,256,8,128]{3,2,1,0:T(8,128)}, f32[4,8,256,128]{3,1,2,0:T(8,128)S(1)}) fusion(f32[32]{0:T(128)S(1)} %get-tuple-element.296, f32[256,4,8,128]{3,2,1,0:T(8,128)} %copy-done.1, s32[32,32768]{1,0:T(8,128)} %param.14), kind=kLoop, calls=%fused_computation.79 | loop fusion | flops 5242880 | bytes 25165952
  113.4 10.0 %fusion.21 = f32[256,4,8,128]{3,2,1,0:T(8,128)S(1)} fusion(f32[4,256,8,128]{3,2,1,0:T(8,128)} %get-tuple-element.394, s32[256,128]{1,0:T(8,128)S(1)} %copy.128, f32[32,256]{0,1:T(8,128)S(1)} %copy.139), kind=kOutput, calls=%fused_computation.42 | convolution fusion | flops 1615855616 | bytes 8552448 | tf_op jit(solution)/shard_map/ebj,bji->ebi/dot_general | solution.py:44
  130.0 10.0 %fusion.20 = f32[256,4,8,128]{3,2,1,0:T(8,128)S(1)} fusion(f32[4,256,8,128]{3,2,1,0:T(8,128)} %get-tuple-element.393, s32[256,128]{1,0:T(8,128)S(1)} %copy.128, f32[32,256]{0,1:T(8,128)S(1)} %copy.144), kind=kOutput, calls=%fused_computation.40 | convolution fusion | flops 1615855616 | bytes 8552448 | tf_op jit(solution)/shard_map/ebj,bji->ebi/dot_general | solution.py:44
  142.7 64.1 %all-reduce.4 = (f32[1024]{0:T(1024)S(1)}, f32[1024]{0:T(1024)S(1)}) all-reduce(f32[1024]{0:T(1024)S(1)} %dynamic-update-slice.1, f32[1024]{0:T(1024)S(1)} %dynamic-update-slice.2), channel_id=3, replica_groups=mesh['ep'=4,'tm'=32] {'tm'}, use_global_device_ids=true, to_apply=%add.2 | all-reduce | flops 2048 | bytes 16384
  206.9 10.2 %convert_bitcast_fusion = (bf16[1,32,1,32768]{3,1,2,0:T(8,128)(2,1)S(1)}, f32[32,32768]{1,0:T(8,128)}, bf16[1,32,1,32768]{3,1,2,0:T(8,128)(2,1)S(1)}, f32[32,32768]{1,0:T(8,128)}) fusion(f32[32]{0:T(128)S(1)} %get-tuple-element.298, f32[256,4,8,128]{3,2,1,0:T(8,128)} %copy-done.2, f32[32]{0:T(128)S(1)} %get-tuple-element.297, f32[256,4,8,128]{3,2,1,0:T(8,128)} %copy-done, ...), kind=kLoop, calls=%fused_computation.52 | loop fusion | flops 10485760 | bytes 29360384 | tf_op jit(solution)/shard_map/stack | solution.py:115
  219.5 33.0 %copy.146 = bf16[2,32,1,32768]{1,0,2,3:T(2,128)(2,1)} copy(bf16[2,32,1,32768]{3,1,2,0:T(8,128)(2,1)} %pad_maximum_fusion) | data formatting | bytes 8388608 | tf_op jit(solution)/shard_map/stack | solution.py:115
  252.5 19.2 %reshape.184 = bf16[4,2,262144]{2,1,0:T(2,128)(2,1)} reshape(bf16[32768,1,2,32]{3,2,1,0:T(2,128)(2,1)} %bitcast.143) | data formatting | bytes 8388608
  271.7 5.3 all-to-all-start
  277.1 117.7 %while.55 = (s32[]{:T(128)}, f32[32,2,64]{2,0,1:T(8,128)S(1)}, s32[32,32768]{1,0:T(8,128)}, f32[32,32768]{1,0:T(8,128)}, f32[32,32768]{1,0:T(8,128)}, /*index=5*/s32[]{:T(128)}, s32[]{:T(128)}, s32[]{:T(128)}, s32[]{:T(128)}) while((s32[]{:T(128)}, f32[32,2,64]{2,0,1:T(8,128)S(1)}, s32[32,32768]{1,0:T(8,128)}, ...), condition=%wide.region_18.19_spmd.clone, body=%wide.region_15.18_spmd.clone.sunk | while | flops 20979716 | bytes 2424997 | solution.py:73
  279.1 5.3 fusion.39
  286.5 5.3 fusion.39
  293.8 5.3 fusion.39
  301.2 5.3 fusion.39
  308.5 5.3 fusion.39
  315.9 5.3 fusion.39
  323.2 5.3 fusion.39
  330.6 5.3 fusion.39
  337.9 5.3 fusion.39
  345.3 5.3 fusion.39
  352.7 5.3 fusion.39
  360.0 5.3 fusion.39
  374.7 5.3 fusion.39
  382.1 5.3 fusion.39
  394.7 124.3 %psum.7 = f32[32,2,64]{2,0,1:T(8,128)S(1)} all-reduce(f32[32,2,64]{2,0,1:T(8,128)S(1)} %get-tuple-element.299), channel_id=1, replica_groups=mesh['ep'=4,'tm'=32] {'tm'}, use_global_device_ids=true, to_apply=%region_19.20 | all-reduce | flops 4096 | bytes 32768 | tf_op jit(solution)/shard_map/psum | solution.py:118
  521.3 80.5 %while.54 = (s32[]{:T(128)}, f32[32,32768]{1,0:T(8,128)}, s32[32,32768]{1,0:T(8,128)}, f32[32,64]{1,0:T(8,128)S(1)}, s32[]{:T(128)}, /*index=5*/s32[]{:T(128)}, s32[]{:T(128)}, s32[]{:T(128)}) while((s32[]{:T(128)}, f32[32,32768]{1,0:T(8,128)}, s32[32,32768]{1,0:T(8,128)}, f32[32,64]{1,0:T(8,128)S(1)}, s32[]{:T(128)}, ...), condition=%wide.region_22.23_spmd.clone, body=%wide.region_20.22_spmd.clone.sunk | while | flops 12517382 | bytes 1581203 | solution.py:89
  601.8 5.9 add.165
  607.7 12.0 %reshape.185 = bf16[32768,1,2,32]{3,2,1,0:T(2,128)(2,1)} reshape(bf16[4,2,262144]{2,1,0:T(2,128)(2,1)} %all-to-all-done) | data formatting | bytes 8388608
  619.7 40.0 %copy.150 = bf16[2,32,1,4,8192]{4,3,1,0,2:T(4,128)(2,1)} copy(bf16[2,32,1,4,8192]{1,0,4,3,2:T(2,128)(2,1)} %bitcast.144) | data formatting | bytes 8388608 | tf_op jit(solution)/shard_map/all_to_all | solution.py:116
  659.8 6.5 copy.148
  (208 shorter events, 156.1 us)
Async XLA Ops:
  0.6 6.2 copy-start.5
  22.6 2.0 copy-start.1
  22.6 2.1 copy-start.6
  123.4 2.1 copy-start
  123.4 3.7 copy-start.3
  140.0 2.0 copy-start.2
  271.7 336.0 %all-to-all-start = ((bf16[4,2,262144]{2,1,0:T(2,128)(2,1)}), bf16[4,2,262144]{2,1,0:T(2,128)(2,1)}, u32[]{:S(2)}, u32[]{:S(2)}) async-start(bf16[4,2,262144]{2,1,0:T(2,128)(2,1)} %reshape.184), calls=%async_computation | async-start | bytes 8388608 | tf_op jit(solution)/shard_map/all_to_all | solution.py:116
  601.8 5.9 copy-start.4
where the time goes:
time: 677 us; the launch traced here: 666 us
  blocking collectives  257 us (38%)
  local copies, waits for them, and re-layouts  195 us (29%)
  other arithmetic  176 us (26%)
  matrix products  30 us (4%)
    unnamed x2, blocking collectives  133 us
    psum x1, blocking collectives, on_device(): totals = lax.psum(partial_value, 'tm')  124 us
    reduce_sum x16, other arithmetic, one_block(): gsum = jnp.sum(jnp.where(hits, part_grad[:, None, :], 0.0), axis=2)  84.3 us
    reduce_sum x16, other arithmetic, one_block(): picked = jnp.sum(jnp.where(hits, table[:, :, None], 0.0), axis=1)  53.2 us
    unnamed x27, local copies, waits for them, and re-layouts  49.8 us
    all_to_all x2, local copies, waits for them, and re-layouts, on_device(): lax.all_to_all(stacked, 'ep', split_axis=3, concat_axis=1, tiled=True)  46.5 us
    another operation x1, local copies, waits for them, and re-layouts, on_device(): jnp.stack([gradient, hessian]).astype(jnp.bfloat16)  33 us
    dynamic_slice x32, local copies, waits for them, and re-layouts, one_block(): part_leaf = lax.dynamic_slice_in_dim(leaf_index, start, width, 1)  31.1 us
  transfers between devices with their start and end apart: 1, of which 0 were waited for; matrix products, arithmetic and copies ran while one was open for 31% of the time, Pallas kernels for 0%

commit v1 on v0

--- a/solution.py
+++ b/solution.py
@@ -113,7 +113,10 @@
     gradient = weight * accum_one - observed
     hessian = weight * accum_one - weight * weight * accum_two
     stacked = jnp.stack([gradient, hessian]).astype(jnp.bfloat16).reshape(2, groups, 1, length)
-    grad_hess = lax.all_to_all(stacked, "ep", split_axis=3, concat_axis=1, tiled=True)
+    grad_hess = jnp.concatenate(
+        lax.all_to_all(jnp.stack(jnp.split(stacked, lax.axis_size("ep"), axis=3)), "ep", 0, 0),
+        axis=1,
+    )
     partial_value = leaf_partials(leaf_index, gradient, hessian, LEAVES)
     totals = lax.psum(partial_value, "tm")
     leaf_weights = -totals[:, 0] / (totals[:, 1] + 1.0)

time: 677 us -> 568 us (0.84)
  local copies, waits for them, and re-layouts: 195 us -> 85.1 us
    all_to_all x2 -> x0, local copies, waits for them, and re-layouts: 46.5 us -> none  [on_device(): lax.all_to_all(stacked, 'ep', split_axis=3, concat_axis=1, tiled=True)]
    unnamed x27 -> x25, local copies, waits for them, and re-layouts: 49.8 us -> 15 us
    another operation x8, local copies, waits for them, and re-layouts: 33.4 us -> 0.55 us  [the longest x1 33 us: on_device(): jnp.stack([gradient, hessian]).astype(jnp.bfloat16)]
  transfers between devices with their start and end apart: 1 -> 1, of which waited for: 0 -> 0; matrix products, arithmetic and copies ran while one was open for 31% -> 37% of each run, Pallas kernels for 0% -> 0%
where the time goes in v1:
time: 568 us; the launch traced here: 558 us
  blocking collectives  257 us (45%)
  other arithmetic  177 us (31%)
  local copies, waits for them, and re-layouts  85.1 us (15%)
  matrix products  30.1 us (5%)
    unnamed x2, blocking collectives  132 us
    psum x1, blocking collectives, on_device(): totals = lax.psum(partial_value, 'tm')  124 us
    reduce_sum x16, other arithmetic, one_block(): gsum = jnp.sum(jnp.where(hits, part_grad[:, None, :], 0.0), axis=2)  84.3 us
    reduce_sum x16, other arithmetic, one_block(): picked = jnp.sum(jnp.where(hits, table[:, :, None], 0.0), axis=1)  53.2 us
    dynamic_slice x32, local copies, waits for them, and re-layouts, one_block(): part_leaf = lax.dynamic_slice_in_dim(leaf_index, start, width, 1)  31.1 us
    dot_general x3, matrix products, block_cumsum(): jnp.einsum('ebj,bji->ebi', shaped, matrices, precision=lax.Precision.HIGH...  30.1 us
    dynamic_slice x16, local copies, waits for them, and re-layouts, one_block(): part_hess = lax.dynamic_slice_in_dim(hessian, start, width, 1)  17.1 us
    unnamed x25, local copies, waits for them, and re-layouts  15 us
  transfers between devices with their start and end apart: 1, of which 0 were waited for; matrix products, arithmetic and copies ran while one was open for 37% of the time, Pallas kernels for 0%

profile of v1, /device:TPU:2, one launch (start us, length us, event | category | flops | bytes accessed | tf_op | source)
XLA Modules:
  0.0 557.7 jit_solution(16512008324978466375)
XLA Ops:
  0.6 4.7 exponential_bitcast_fusion.1
  9.0 10.0 %fusion.23 = f32[256,4,8,128]{3,2,1,0:T(8,128)S(1)} fusion(f32[4,256,8,128]{3,2,1,0:T(8,128)} %get-tuple-element.397, s32[256,128]{1,0:T(8,128)S(1)} %copy.68, f32[32,256]{0,1:T(8,128)S(1)} %copy.72), kind=kOutput, calls=%fused_computation.48 | convolution fusion | flops 1615855616 | bytes 8552448 | tf_op jit(solution)/shard_map/ebj,bji->ebi/dot_general | solution.py:44
  22.6 68.6 %all-reduce.1 = f32[1024]{0:T(1024)S(1)} all-reduce(f32[1024]{0:T(1024)S(1)} %dynamic-update-slice), channel_id=2, replica_groups=mesh['ep'=4,'tm'=32] {'tm'}, use_global_device_ids=true, to_apply=%add.1 | all-reduce | flops 1024 | bytes 8192
  92.6 9.4 %fusion.37 = (f32[4,8,256,128]{3,1,2,0:T(8,128)S(1)}, f32[4,256,8,128]{3,2,1,0:T(8,128)}, f32[4,256,8,128]{3,2,1,0:T(8,128)}, f32[4,8,256,128]{3,1,2,0:T(8,128)}) fusion(f32[32]{0:T(128)S(1)} %get-tuple-element.296, f32[256,4,8,128]{3,2,1,0:T(8,128)} %copy-done.2, s32[32,32768]{1,0:T(8,128)} %param.14), kind=kLoop, calls=%fused_computation.88 | loop fusion | flops 5242880 | bytes 25165952
  105.6 4.4 reduce_window_min.10
  110.1 10.0 %fusion.21 = f32[256,4,8,128]{3,2,1,0:T(8,128)S(1)} fusion(f32[4,256,8,128]{3,2,1,0:T(8,128)} %get-tuple-element.390, s32[256,128]{1,0:T(8,128)S(1)} %copy.66, f32[32,256]{0,1:T(8,128)S(1)} %copy.82), kind=kOutput, calls=%fused_computation.44 | convolution fusion | flops 1615855616 | bytes 8552448 | tf_op jit(solution)/shard_map/ebj,bji->ebi/dot_general | solution.py:44
  126.7 10.2 %fusion.22 = f32[256,4,8,128]{3,2,1,0:T(8,128)S(1)} fusion(f32[4,256,8,128]{3,2,1,0:T(8,128)} %get-tuple-element.391, s32[256,128]{1,0:T(8,128)S(1)} %copy.66, f32[32,256]{0,1:T(8,128)S(1)} %copy.77), kind=kOutput, calls=%fused_computation.46 | convolution fusion | flops 1615855616 | bytes 8552448 | tf_op jit(solution)/shard_map/ebj,bji->ebi/dot_general | solution.py:44
  139.5 63.7 %all-reduce.4 = (f32[1024]{0:T(1024)S(1)}, f32[1024]{0:T(1024)S(1)}) all-reduce(f32[1024]{0:T(1024)S(1)} %dynamic-update-slice.1, f32[1024]{0:T(1024)S(1)} %dynamic-update-slice.2), channel_id=3, replica_groups=mesh['ep'=4,'tm'=32] {'tm'}, use_global_device_ids=true, to_apply=%add.2 | all-reduce | flops 2048 | bytes 16384
  203.4 10.3 %convert_bitcast_fusion = (bf16[1,32,1,32768]{3,1,2,0:T(8,128)(2,1)S(1)}, f32[32,32768]{1,0:T(8,128)}, bf16[1,32,1,32768]{3,1,2,0:T(8,128)(2,1)S(1)}, f32[32,32768]{1,0:T(8,128)}) fusion(f32[32]{0:T(128)S(1)} %get-tuple-element.298, f32[256,4,8,128]{3,2,1,0:T(8,128)} %copy-done, f32[32]{0:T(128)S(1)} %get-tuple-element.297, f32[256,4,8,128]{3,2,1,0:T(8,128)} %copy-done.1, ...), kind=kLoop, calls=%fused_computation.56 | loop fusion | flops 10485760 | bytes 29360384 | tf_op jit(solution)/shard_map/stack | solution.py:115
  216.6 5.6 all-to-all-start
  222.2 117.7 %while.55 = (s32[]{:T(128)}, f32[32,2,64]{2,0,1:T(8,128)S(1)}, s32[32,32768]{1,0:T(8,128)}, f32[32,32768]{1,0:T(8,128)}, f32[32,32768]{1,0:T(8,128)}, /*index=5*/s32[]{:T(128)}, s32[]{:T(128)}, s32[]{:T(128)}, s32[]{:T(128)}) while((s32[]{:T(128)}, f32[32,2,64]{2,0,1:T(8,128)S(1)}, s32[32,32768]{1,0:T(8,128)}, ...), condition=%wide.region_18.19_spmd.clone, body=%wide.region_15.18_spmd.clone.sunk | while | flops 20979716 | bytes 2424989 | solution.py:73
  224.2 5.3 fusion.42
  231.6 5.3 fusion.42
  238.9 5.3 fusion.42
  246.3 5.3 fusion.42
  253.7 5.3 fusion.42
  261.0 5.3 fusion.42
  268.4 5.3 fusion.42
  275.7 5.3 fusion.42
  283.1 5.3 fusion.42
  290.4 5.3 fusion.42
  297.8 5.3 fusion.42
  305.1 5.3 fusion.42
  312.5 5.3 fusion.42
  319.9 5.3 fusion.42
  327.2 5.3 fusion.42
  334.6 5.3 fusion.42
  339.9 124.3 %psum.7 = f32[32,2,64]{2,0,1:T(8,128)S(1)} all-reduce(f32[32,2,64]{2,0,1:T(8,128)S(1)} %get-tuple-element.299), channel_id=1, replica_groups=mesh['ep'=4,'tm'=32] {'tm'}, use_global_device_ids=true, to_apply=%region_19.20 | all-reduce | flops 4096 | bytes 32768 | tf_op jit(solution)/shard_map/psum | solution.py:121
  466.5 80.5 %while.54 = (s32[]{:T(128)}, f32[32,32768]{1,0:T(8,128)}, s32[32,32768]{1,0:T(8,128)}, f32[32,64]{1,0:T(8,128)S(1)}, s32[]{:T(128)}, /*index=5*/s32[]{:T(128)}, s32[]{:T(128)}, s32[]{:T(128)}) while((s32[]{:T(128)}, f32[32,32768]{1,0:T(8,128)}, s32[32,32768]{1,0:T(8,128)}, f32[32,64]{1,0:T(8,128)S(1)}, s32[]{:T(128)}, ...), condition=%wide.region_22.23_spmd.clone, body=%wide.region_20.22_spmd.clone.sunk | while | flops 12517382 | bytes 1581195 | solution.py:89
  467.4 3.3 select_reduce_fusion.2
  546.9 5.9 %add.165 = f32[32,32768]{1,0:T(8,128)} add(f32[32,32768]{1,0:T(8,128)} %param.12, f32[32,32768]{1,0:T(8,128)} %get-tuple-element.300) | non-fusion elementwise | flops 1048576 | bytes 12582912 | tf_op jit(solution)/shard_map/add | solution.py:123
  552.8 4.6 copy.87
  (207 shorter events, 136.5 us)
Async XLA Ops:
  6.1 2.5 copy-start.5
  19.0 2.0 copy-start.2
  19.0 2.1 copy-start.6
  120.1 2.1 copy-start
  120.1 3.7 copy-start.3
  136.9 2.0 copy-start.1
  216.6 336.2 %all-to-all-start = ((bf16[4,2,32,1,8192]{4,2,1,3,0:T(8,128)(2,1)}), bf16[4,2,32,1,8192]{4,2,1,3,0:T(8,128)(2,1)}, u32[]{:S(2)}, u32[]{:S(2)}) async-start(bf16[4,2,32,1,8192]{4,2,1,3,0:T(8,128)(2,1)} %pad_maximum_fusion.1), calls=%async_computation | async-start | bytes 8388608 | tf_op jit(solution)/shard_map/all_to_all | solution.py:117
  546.9 5.9 %copy-start.4 = (f32[32,64]{1,0:T(8,128)}, f32[32,64]{1,0:T(8,128)S(1)}, u32[]{:S(2)}) copy-start(f32[32,64]{1,0:T(8,128)S(1)} %get-tuple-element.635) | copy-start | bytes 24580
